TPU v7x, 128 devices: a whole 4x4x4 slice. The times are simulated.
128 devices in a mesh: seq: 8 (over z, core), exp: 16 (over x, y).
Axes of the slice: x: 4, y: 4, z: 4, core: 2. Of those that a mesh axis runs over, the one named last changes fastest.
Arguments:
- residual: bfloat16 [16384, 8192], P(('seq', 'exp')), may hold values from -6 to 6
- expert_rows: bfloat16 [8, 16, 16, 24, 8192], P('seq', 'exp'), may hold values from -6 to 6
- expert_ids: int32 [16384, 2], P(('seq', 'exp')), may hold values from 0 to 15, as said below
- expert_slots: int32 [16384, 2], P(('seq', 'exp')), may hold values from 0 to 23, as said below
- combine_weights: float32 [16384, 2], P(('seq', 'exp')), may hold values from 0.1 to 0.9
- norm_gain: float32 [8192], replicated, may hold values from 0.1 to 1.9
- in_weight: bfloat16 [8192, 8192], P(None, 'exp'), may hold values from -0.0625 to 0.0625
- conv_weight: float32 [4, 8192], P(None, 'exp'), may hold values from -3 to 3
- conv_bias: float32 [8192], P('exp'), may hold values from -0.5 to 0.5
- bc_weight: bfloat16 [8192, 128], P('exp'), may hold values from -0.00390625 to 0.00390625
- dt_weight: bfloat16 [8192, 128], P('exp'), may hold values from -0.0625 to 0.0625
- dt_bias: float32 [128], P('exp'), may hold values from -2 to 0.5
- decay_log: float32 [128], P('exp'), may hold values from -14 to -3.2
- skip_gain: float32 [128], P('exp'), may hold values from -1 to 3
Outputs:
- scan_output: bfloat16 [16384, 8192], P('seq', 'exp')
Inputs may be any that keep to these rules, and one draw needn't show every extreme that they name: `expert_ids`: A token's two ids differ. The tokens of one device name no expert more than 24 times, and in each span one expert is named exactly 24 times by the tokens of every device of the span. `expert_slots`: A token's slot at its k-th expert counts the earlier (token, k) pairs of the same device, in row-major order, that name the same expert.
All inputs are finite; a program needn't handle non-finite values.
Results may differ from a plain program's by a relative error of at most 0.0074.
Values may be sent and summed in bfloat16 or wider, within the bound.
No kernel may reach another device: no remote copies, remote signals or barrier semaphores. Data moves between devices by JAX's collectives and lax.ppermute only.
A program may use at most 320 MiB of HBM per device.

v0:
```python
import jax
import jax.numpy as jnp
from jax import lax
from jax.sharding import PartitionSpec as P

TOPK = 2
KCONV = 4
HEAD = 64
NSTATE = 64
STRETCH = 256


def passed_along(value, axis, steps):
    count = lax.axis_size(axis)
    leading, last = (max(0, -steps), min(count, count - steps))
    return lax.ppermute(value, axis, [(source, source + steps) for source in range(leading, last)])


def block_terms(b_rows, c_rows, steps_dt, decays, values):
    running = jnp.cumsum(decays, axis=0)
    scores = jnp.dot(c_rows, b_rows.T, preferred_element_type=jnp.float32)
    length = running.shape[0]
    causal = (jnp.arange(length)[:, None] >= jnp.arange(length)[None, :])[:, :, None]
    decay_gap = jnp.where(causal, running[:, None, :] - running[None, :, :], 0.0)
    mixing = jnp.where(
        causal, jnp.exp(decay_gap) * scores[:, :, None] * steps_dt[None, :, :], 0.0
    ).astype(jnp.bfloat16)
    inside = jnp.einsum("tsh,shp->thp", mixing, values, preferred_element_type=jnp.float32)
    carried = jnp.exp(running[-1][None, :] - running) * steps_dt
    states = jnp.einsum(
        "sn,shp->hnp",
        b_rows.astype(jnp.float32),
        carried[:, :, None] * values.astype(jnp.float32),
        precision=lax.Precision.HIGHEST,
    )
    return (running, inside, states, jnp.exp(running[-1]))


def shards(
    residual,
    expert_rows,
    expert_ids,
    expert_slots,
    combine_weights,
    norm_gain,
    in_weight,
    conv_weight,
    conv_bias,
    bc_weight,
    dt_weight,
    dt_bias,
    decay_log,
    skip_gain,
):
    own_rows, width = residual.shape
    returned = lax.all_to_all(expert_rows, "exp", split_axis=2, concat_axis=1, tiled=True)
    capacity = returned.shape[3]
    buffers = returned.reshape(returned.shape[1] * capacity, width)
    picked = jnp.take(buffers, expert_ids * capacity + expert_slots, axis=0)
    mixture = jnp.zeros((own_rows, width), jnp.float32)
    for column in range(TOPK):
        mixture = mixture + combine_weights[:, column][:, None] * picked[:, column].astype(
            jnp.float32
        )
    stream = residual.astype(jnp.float32) + mixture
    factor = lax.rsqrt(jnp.mean(stream * stream, axis=1, keepdims=True) + 1e-06)
    normed = (stream * factor * norm_gain[None, :]).astype(jnp.bfloat16)
    group_rows = own_rows * lax.axis_size("exp")
    local_width = in_weight.shape[1]
    x_in = jnp.dot(
        lax.all_gather(normed, "exp", axis=0, tiled=True),
        in_weight,
        preferred_element_type=jnp.float32,
    ).astype(jnp.bfloat16)
    rim_rows = passed_along(x_in[group_rows - (KCONV - 1) :], "seq", 1)
    padded = jnp.concatenate([rim_rows, x_in], axis=0)
    filtered = jnp.zeros((group_rows, local_width), jnp.float32) + conv_bias[None, :]
    for tap in range(KCONV):
        filtered = filtered + conv_weight[tap][None, :] * padded[tap : tap + group_rows].astype(
            jnp.float32
        )
    activated = jax.nn.silu(filtered).astype(jnp.bfloat16)
    state_part = jnp.dot(activated, bc_weight, preferred_element_type=jnp.float32)
    rate_part = jnp.dot(activated, dt_weight, preferred_element_type=jnp.float32)
    state_proj, dt_raw = lax.psum((state_part, rate_part), "exp")
    heads_here = local_width // HEAD
    first_head = lax.axis_index("exp") * heads_here
    steps_dt = jax.nn.softplus(
        lax.dynamic_slice_in_dim(dt_raw, first_head, heads_here, 1) + dt_bias[None, :]
    )
    decays = -jnp.exp(decay_log)[None, :] * steps_dt
    b_all = state_proj[:, :NSTATE].astype(jnp.bfloat16)
    c_all = state_proj[:, NSTATE:].astype(jnp.bfloat16)
    blocks = group_rows // STRETCH
    c_blocks = c_all.reshape(blocks, STRETCH, NSTATE)
    value_blocks = activated.reshape(blocks, STRETCH, heads_here, HEAD)

    def advance(carry, inputs):
        local_states, prefix_decay = carry
        b_rows, c_rows, block_dt, block_decays, values = inputs
        running, inside, states, total = block_terms(b_rows, c_rows, block_dt, block_decays, values)
        return (
            (total[:, None, None] * local_states + states, prefix_decay * total),
            (running, inside, local_states, prefix_decay),
        )

    start_carry = (
        jnp.zeros((heads_here, NSTATE, HEAD), jnp.float32),
        jnp.ones((heads_here,), jnp.float32),
    )
    (final_states, device_decay), (runnings, insides, starts, prefixes) = lax.scan(
        advance,
        start_carry,
        (
            b_all.reshape(blocks, STRETCH, NSTATE),
            c_blocks,
            steps_dt.reshape(blocks, STRETCH, heads_here),
            decays.reshape(blocks, STRETCH, heads_here),
            value_blocks,
        ),
    )
    empty_states = jnp.zeros((heads_here, NSTATE, HEAD), jnp.float32)

    def relay_turn(turn, carried):
        incoming, outgoing = carried
        incoming = passed_along(outgoing, "seq", 1)
        return (incoming, device_decay[:, None, None] * incoming + final_states)

    incoming, outgoing_last = lax.fori_loop(
        0, lax.axis_size("seq") - 1, relay_turn, (empty_states, final_states)
    )
    entering = starts + prefixes[:, :, None, None] * incoming[None]
    across = jnp.exp(runnings)[:, :, :, None] * jnp.einsum(
        "btn,bhnp->bthp", c_blocks.astype(jnp.float32), entering, precision=lax.Precision.HIGHEST
    )
    output = insides + across + skip_gain[None, None, :, None] * value_blocks.astype(jnp.float32)
    return output.astype(jnp.bfloat16).reshape(group_rows, local_width)


def solution(mesh):
    placed = (
        P(("seq", "exp"), None),
        P("seq", "exp", None, None, None),
        P(("seq", "exp"), None),
        P(("seq", "exp"), None),
        P(("seq", "exp"), None),
        P(),
        P(None, "exp"),
        P(None, "exp"),
        P("exp"),
        P("exp", None),
        P("exp", None),
        P("exp"),
        P("exp"),
        P("exp"),
    )
    return jax.shard_map(
        shards, mesh=mesh, in_specs=placed, out_specs=P("seq", "exp"), check_vma=False
    )
```

profile of v0, /device:TPU:1, one launch (start us, length us, event | category | flops | bytes accessed | tf_op | source)
XLA Modules:
  0.0 613.9 jit_solution(3130771036729045118)
XLA Ops:
  6.5 7.8 %all-to-all-start = ((bf16[1,1,16,24,8192]{4,3,1,0,2:T(8,128)(2,1)}), bf16[1,1,16,24,8192]{4,3,1,0,2:T(8,128)(2,1)}, u32[]{:S(2)}, u32[]{:S(2)}) async-start(bf16[1,1,16,24,8192]{4,3,1,0,2:T(8,128)(2,1)} %bitcast.113), calls=%async_computation | async-start | bytes 12582912 | tf_op jit(solution)/shard_map/all_to_all | solution.py:56
  14.7 100.4 %all-to-all-done = bf16[1,1,16,24,8192]{4,3,1,0,2:T(8,128)(2,1)} async-done(((bf16[1,1,16,24,8192]{4,3,1,0,2:T(8,128)(2,1)}), bf16[1,1,16,24,8192]{4,3,1,0,2:T(8,128)(2,1)}, u32[]{:S(2)}, u32[]{:S(2)}) %all-to-all-start) | async-done | bytes 6291488 | tf_op jit(solution)/shard_map/all_to_all | solution.py:56
  115.1 12.6 %gather_fusion = bf16[256,8192]{1,0:T(8,128)(2,1)} fusion(bf16[384,8192]{1,0:T(8,128)(2,1)} %bitcast.3, s32[1024]{0:T(1024)S(1)} %pad_clamp_fusion), kind=kCustom, calls=%fused_computation | custom fusion | bytes 8389632 | tf_op jit(solution)/shard_map/jit(_take)/gather | solution.py:59
  127.7 7.6 %reshape.94 = bf16[128,2,8192]{2,1,0:T(2,128)(2,1)} reshape(bf16[256,8192]{1,0:T(8,128)(2,1)} %gather_fusion) | data formatting | bytes 8388608 | tf_op jit(solution)/shard_map/jit(_take)/gather | solution.py:59
  135.3 7.2 %copy_select_fusion = bf16[128,2,8192]{2,0,1:T(8,128)(2,1)S(1)} fusion(bf16[128,2,8192]{2,1,0:T(2,128)(2,1)} %reshape.94, pred[128,2]{0,1:T(4,128)(4,1)S(1)} %get-tuple-element.250), kind=kLoop, calls=%fused_computation.47 | loop fusion | flops 2097152 | bytes 8388864 | tf_op jit(solution)/shard_map/jit(_take)/select_n | solution.py:59
  142.6 1.4 multiply_reduce_fusion
  144.0 3.0 multiply_convert_fusion.1
  147.1 205.3 %all-gather.2.cloned.1.call-done = bf16[2048,8192]{1,0:T(8,128)(2,1)} async-done(((bf16[128,8192]{1,0:T(8,128)(2,1)}), bf16[2048,8192]{1,0:T(8,128)(2,1)}) %all-gather.2.cloned.1.call-update) | async-done | bytes 33554448 | tf_op jit(solution)/shard_map/all_gather | solution.py:71
  352.4 23.7 %convolution_convert_fusion = bf16[2048,512]{1,0:T(8,128)(2,1)S(1)} fusion(bf16[2048,8192]{1,0:T(8,128)(2,1)} %all-gather.2.cloned.1.call-done, bf16[8192,512]{1,0:T(8,128)(2,1)} %param.24), kind=kOutput, calls=%fused_computation.52 | convolution fusion | flops 17180917760 | bytes 44040192 | tf_op jit(solution)/shard_map/dot_general | solution.py:70
  376.2 1.3 copy-done.4
  377.5 3.7 collective-permute-start.1
  382.0 6.0 multiply_convert_fusion
  388.0 1.8 fusion.34
  389.8 1.7 fusion.35
  391.5 3.6 reshape.109
  395.2 4.0 copy.57
  399.2 75.3 %all-reduce.4 = bf16[2048,128]{1,0:T(8,128)(2,1)S(1)} all-reduce(f32[2048,128]{1,0:T(8,128)} %fusion.35), channel_id=1, replica_groups=mesh['seq'=8,'exp'=16] {'exp'}, use_global_device_ids=true, to_apply=%region_1.2 | all-reduce | flops 262144 | bytes 1572864 | tf_op jit(solution)/shard_map/psum | solution.py:85
  475.5 1.2 copy.58
  477.9 38.5 %while.34 = (s32[]{:T(128)}, f32[8,64,64]{1,2,0:T(8,128)S(1)}, f32[8]{0:T(128)S(1)}, f32[8,256,8]{1,2,0:T(8,128)}, f32[8,256,8,64]{1,3,2,0:T(8,128)}, /*index=5*...) while((s32[]{:T(128)}, f32[8,64,64]{1,2,0:T(8,128)S(1)}, ...), condition=%wide.region_6.7_spmd.clone, body=%wide.region_3.6_spmd.clone.sunk | while | flops 180033568 | bytes 2758157 | solution.py:111
  479.3 1.6 fusion.62
  484.1 1.6 fusion.62
  488.9 1.6 fusion.62
  493.7 1.6 fusion.62
  498.5 1.6 fusion.62
  503.3 1.6 fusion.62
  508.1 1.6 fusion.62
  513.0 1.5 fusion.62
  516.6 71.0 %while.33 = (s32[]{:T(128)}, f32[8,64,64]{2,1,0:T(8,128)}, f32[8,64,64]{2,1,0:T(8,128)S(1)}, f32[8]{0:T(128)S(1)}, f32[8,64,64]{2,1,0:T(8,128)S(1)}, /*index=5*/s32[]{:T(128)}) while((s32[]{:T(128)}, f32[8,64,64]{2,1,0:T(8,128)}, f32[8,64,64]{2,1,0:T(8,128)S(1)}, f32[8]{0:T(128)S(1)}, f32[8,64,64]{2,1,0:T(8,128)S(1)}, ...), condition=%wide.region_8.9_spmd, body=%wide.region_7.8_spmd.sunk | while | flops 65538 | bytes 1441961 | solution.py:129
  516.6 16.7 %collective-permute-start = (f32[8,64,64]{2,1,0:T(8,128)S(1)}, f32[8,64,64]{2,1,0:T(8,128)S(1)}, u32[]{:S(2)}, u32[]{:S(2)}) collective-permute-start(f32[8,64,64]{2,1,0:T(8,128)S(1)} %get-tuple-element.428), channel_id=1, source_target_pairs={{0,16},{16,32},{32,48},{48,64},{64,80},{80,96},{96,112},{1,17},{17... | collective-permute-start | bytes 393224 | tf_op jit(solution)/shard_map/while/body/eval_jaxpr/ppermute | solution.py:16
  533.3 3.3 collective-permute-done
  537.3 4.4 collective-permute-start
  541.7 3.3 collective-permute-done
  545.7 4.4 collective-permute-start
  550.1 3.3 collective-permute-done
  554.1 4.4 collective-permute-start
  558.5 3.3 collective-permute-done
  562.5 4.4 collective-permute-start
  566.8 3.3 collective-permute-done
  570.8 4.4 collective-permute-start
  575.2 3.3 collective-permute-done
  579.2 4.4 collective-permute-start
  583.6 3.3 collective-permute-done
  587.6 1.1 copy.61
  588.7 1.8 multiply_add_fusion.1
  590.5 1.8 fusion.36
  592.7 2.8 add_convert_fusion
  595.6 5.1 copy.67
  600.6 6.4 %reshape.108 = bf16[2048,512]{1,0:T(8,128)(2,1)} reshape(bf16[8,256,8,64]{3,2,1,0:T(8,128)(2,1)} %copy.67) | data formatting | bytes 4194304 | tf_op jit(solution)/shard_map/reshape | solution.py:137
  (197 shorter events, 34.4 us)
Async XLA Ops:
  6.5 381.5 %copy-start = (bf16[512,128]{1,0:T(8,128)(2,1)S(1)}, bf16[512,128]{1,0:T(8,128)(2,1)}, u32[]{:S(2)}) copy-start(bf16[512,128]{1,0:T(8,128)(2,1)} %param.28) | copy-start | bytes 393220
  6.5 7.8 %copy-start.10 = (s32[128,2]{0,1:T(2,128)S(1)}, s32[128,2]{0,1:T(2,128)}, u32[]{:S(2)}) copy-start(s32[128,2]{0,1:T(2,128)} %param.21) | copy-start | bytes 3076
  6.5 7.8 %copy-start.11 = (s32[128,2]{0,1:T(2,128)S(1)}, s32[128,2]{0,1:T(2,128)}, u32[]{:S(2)}) copy-start(s32[128,2]{0,1:T(2,128)} %param.20) | copy-start | bytes 3076
  6.5 8.1 %copy-start.12 = (f32[128,2]{0,1:T(2,128)S(1)}, f32[128,2]{0,1:T(2,128)}, u32[]{:S(2)}) copy-start(f32[128,2]{0,1:T(2,128)} %param.22) | copy-start | bytes 3076
  6.5 108.6 %all-to-all-start = ((bf16[1,1,16,24,8192]{4,3,1,0,2:T(8,128)(2,1)}), bf16[1,1,16,24,8192]{4,3,1,0,2:T(8,128)(2,1)}, u32[]{:S(2)}, u32[]{:S(2)}) async-start(bf16[1,1,16,24,8192]{4,3,1,0,2:T(8,128)(2,1)} %bitcast.113), calls=%async_computation | async-start | bytes 12582912 | tf_op jit(solution)/shard_map/all_to_all | solution.py:56
  14.3 338.1 %all-gather.2.cloned.1.call-start = ((), (), s32[]{:S(2)}) async-start(), calls=%async_computation.1 | async-start | bytes 35651584 | tf_op jit(solution)/shard_map/all_gather | solution.py:71
  135.3 7.2 %copy-start.2 = (bf16[128,8192]{1,0:T(8,128)(2,1)S(1)}, bf16[128,8192]{1,0:T(8,128)(2,1)}, u32[]{:S(2)}) copy-start(bf16[128,8192]{1,0:T(8,128)(2,1)} %param.18) | copy-start | bytes 6291460
  142.5 1.4 copy-start.7
  144.0 3.1 copy-start.8
  147.0 330.0 %all-reduce.3.cloned.1.call-start = ((), (), s32[]{:S(2)}) async-start(), calls=%async_computation.2 | async-start | bytes 2097152 | tf_op jit(solution)/shard_map/psum | solution.py:85
  147.1 234.2 %copy-start.15 = (f32[8]{0:T(128)S(1)}, f32[8]{0:T(128)}, u32[]{:S(2)}) copy-start(f32[8]{0:T(128)} %param.30) | copy-start | bytes 100
  147.1 234.9 %copy-start.9 = (f32[512]{0:T(512)S(1)}, f32[512]{0:T(512)}, u32[]{:S(2)}) copy-start(f32[512]{0:T(512)} %param.26) | copy-start | bytes 6148
  376.2 1.3 copy-start.4
  377.5 4.5 collective-permute-start.1
  382.0 7.8 %copy-start.5 = (bf16[512,128]{1,0:T(8,128)(2,1)S(1)}, bf16[512,128]{1,0:T(8,128)(2,1)}, u32[]{:S(2)}) copy-start(bf16[512,128]{1,0:T(8,128)(2,1)} %param.27) | copy-start | bytes 393220
  395.2 81.8 %copy-start.13 = (f32[8]{0:T(128)S(1)}, f32[8]{0:T(128)}, u32[]{:S(2)}) copy-start(f32[8]{0:T(128)} %param.29) | copy-start | bytes 100
  516.6 20.0 %collective-permute-start = (f32[8,64,64]{2,1,0:T(8,128)S(1)}, f32[8,64,64]{2,1,0:T(8,128)S(1)}, u32[]{:S(2)}, u32[]{:S(2)}) collective-permute-start(f32[8,64,64]{2,1,0:T(8,128)S(1)} %get-tuple-element.428), channel_id=1, source_target_pairs={{0,16},{16,32},{32,48},{48,64},{64,80},{80,96},{96,112},{1,17},{17... | collective-permute-start | bytes 393224 | tf_op jit(solution)/shard_map/while/body/eval_jaxpr/ppermute | solution.py:16
  536.6 0.7 copy-start.1
  537.3 7.7 %collective-permute-start = (f32[8,64,64]{2,1,0:T(8,128)S(1)}, f32[8,64,64]{2,1,0:T(8,128)S(1)}, u32[]{:S(2)}, u32[]{:S(2)}) collective-permute-start(f32[8,64,64]{2,1,0:T(8,128)S(1)} %get-tuple-element.428), channel_id=1, source_target_pairs={{0,16},{16,32},{32,48},{48,64},{64,80},{80,96},{96,112},{1,17},{17... | collective-permute-start | bytes 393224 | tf_op jit(solution)/shard_map/while/body/eval_jaxpr/ppermute | solution.py:16
  545.0 0.7 copy-start.1
  545.7 7.7 %collective-permute-start = (f32[8,64,64]{2,1,0:T(8,128)S(1)}, f32[8,64,64]{2,1,0:T(8,128)S(1)}, u32[]{:S(2)}, u32[]{:S(2)}) collective-permute-start(f32[8,64,64]{2,1,0:T(8,128)S(1)} %get-tuple-element.428), channel_id=1, source_target_pairs={{0,16},{16,32},{32,48},{48,64},{64,80},{80,96},{96,112},{1,17},{17... | collective-permute-start | bytes 393224 | tf_op jit(solution)/shard_map/while/body/eval_jaxpr/ppermute | solution.py:16
  553.4 0.7 copy-start.1
  554.1 7.7 %collective-permute-start = (f32[8,64,64]{2,1,0:T(8,128)S(1)}, f32[8,64,64]{2,1,0:T(8,128)S(1)}, u32[]{:S(2)}, u32[]{:S(2)}) collective-permute-start(f32[8,64,64]{2,1,0:T(8,128)S(1)} %get-tuple-element.428), channel_id=1, source_target_pairs={{0,16},{16,32},{32,48},{48,64},{64,80},{80,96},{96,112},{1,17},{17... | collective-permute-start | bytes 393224 | tf_op jit(solution)/shard_map/while/body/eval_jaxpr/ppermute | solution.py:16
  561.8 0.7 copy-start.1
  562.5 7.7 %collective-permute-start = (f32[8,64,64]{2,1,0:T(8,128)S(1)}, f32[8,64,64]{2,1,0:T(8,128)S(1)}, u32[]{:S(2)}, u32[]{:S(2)}) collective-permute-start(f32[8,64,64]{2,1,0:T(8,128)S(1)} %get-tuple-element.428), channel_id=1, source_target_pairs={{0,16},{16,32},{32,48},{48,64},{64,80},{80,96},{96,112},{1,17},{17... | collective-permute-start | bytes 393224 | tf_op jit(solution)/shard_map/while/body/eval_jaxpr/ppermute | solution.py:16
  570.1 0.7 copy-start.1
  570.8 7.7 %collective-permute-start = (f32[8,64,64]{2,1,0:T(8,128)S(1)}, f32[8,64,64]{2,1,0:T(8,128)S(1)}, u32[]{:S(2)}, u32[]{:S(2)}) collective-permute-start(f32[8,64,64]{2,1,0:T(8,128)S(1)} %get-tuple-element.428), channel_id=1, source_target_pairs={{0,16},{16,32},{32,48},{48,64},{64,80},{80,96},{96,112},{1,17},{17... | collective-permute-start | bytes 393224 | tf_op jit(solution)/shard_map/while/body/eval_jaxpr/ppermute | solution.py:16
  578.5 0.7 copy-start.1
  579.2 7.7 %collective-permute-start = (f32[8,64,64]{2,1,0:T(8,128)S(1)}, f32[8,64,64]{2,1,0:T(8,128)S(1)}, u32[]{:S(2)}, u32[]{:S(2)}) collective-permute-start(f32[8,64,64]{2,1,0:T(8,128)S(1)} %get-tuple-element.428), channel_id=1, source_target_pairs={{0,16},{16,32},{32,48},{48,64},{64,80},{80,96},{96,112},{1,17},{17... | collective-permute-start | bytes 393224 | tf_op jit(solution)/shard_map/while/body/eval_jaxpr/ppermute | solution.py:16
  586.9 0.7 copy-start.1
  590.5 1.9 copy-start.6
  590.5 2.2 copy-start.3
  590.5 2.2 copy-start.14
Sparse Core Ops, SparseCore 0:
  147.1 205.2 all-gather.1
  390.0 86.9 all-reduce.2
where the time goes:
time: 615 us; the launch traced here: 614 us
  waiting for transfers between devices  330 us (54%)
  blocking collectives  75.3 us (12%)
  starting transfers between devices  54.6 us (9%)
  local copies, waits for them, and re-layouts  52.2 us (8%)
  matrix products  46.7 us (8%)
  other arithmetic  41.4 us (7%)
  between operations  13.8 us (2%)
    all_gather x1, waiting for transfers between devices, shards(): lax.all_gather(normed, 'exp', axis=0, tiled=True)  205 us
    all_to_all x1, waiting for transfers between devices, shards(): lax.all_to_all(expert_rows, 'exp', split_axis=2, concat_axis=1, tiled=True)  100 us
    psum x1, blocking collectives, shards(): state_proj, dt_raw = lax.psum((state_part, rate_part), 'exp')  75.3 us
    ppermute x8, starting transfers between devices, passed_along(): lax.ppermute(value, axis, [(source, source + steps) for source in range(l...  46.7 us
    dot_general x1, matrix products, shards(): jnp.dot(lax.all_gather(normed, 'exp', axis=0, tiled=True), in_weight, pre...  23.7 us
    ppermute x8, waiting for transfers between devices, passed_along(): lax.ppermute(value, axis, [(source, source + steps) for source in range(l...  23.7 us
    gather x2, local copies, waits for them, and re-layouts, shards(): picked = jnp.take(buffers, expert_ids * capacity + expert_slots, axis=0)  20.2 us
    dot_general x8, matrix products, block_terms(): jnp.einsum('tsh,shp->thp', mixing, values, preferred_element_type=jnp.flo...  12.5 us
  transfers between devices with their start and end apart: 11, of which 11 were waited for; matrix products, arithmetic and copies ran while one was open for 2% of the time, Pallas kernels for 0%

commit v1 on v0

--- a/solution.py
+++ b/solution.py
@@ -8,6 +8,28 @@
 HEAD = 64
 NSTATE = 64
 STRETCH = 256
+
+
+def laid_out(blocks, dim):
+    dims = list(blocks.shape[1:])
+    dims[dim] *= blocks.shape[0]
+    return jnp.moveaxis(blocks, 0, dim).reshape(dims)
+
+
+def collect(array, axis, dim):
+    size = lax.axis_size(axis)
+    pairs = [(i, (i + 1) % size) for i in range(size)]
+    back = [(b, a) for a, b in pairs]
+    lower, upper = ([], [])
+    for step in range(size - 1):
+        if step % 2 == 0:
+            lower.append(lax.ppermute(lower[-1] if lower else array, axis, pairs))
+        else:
+            upper.append(lax.ppermute(upper[-1] if upper else array, axis, back))
+    parts = jnp.stack([*lower[::-1], array, *upper])
+    shift = lax.axis_index(axis) - len(lower)
+    parts = parts[(jnp.arange(size) - shift) % size]
+    return laid_out(parts, dim)
 
 
 def passed_along(value, axis, steps):
@@ -67,11 +89,9 @@
     normed = (stream * factor * norm_gain[None, :]).astype(jnp.bfloat16)
     group_rows = own_rows * lax.axis_size("exp")
     local_width = in_weight.shape[1]
-    x_in = jnp.dot(
-        lax.all_gather(normed, "exp", axis=0, tiled=True),
-        in_weight,
-        preferred_element_type=jnp.float32,
-    ).astype(jnp.bfloat16)
+    x_in = jnp.dot(collect(normed, "exp", 0), in_weight, preferred_element_type=jnp.float32).astype(
+        jnp.bfloat16
+    )
     rim_rows = passed_along(x_in[group_rows - (KCONV - 1) :], "seq", 1)
     padded = jnp.concatenate([rim_rows, x_in], axis=0)
     filtered = jnp.zeros((group_rows, local_width), jnp.float32) + conv_bias[None, :]

time: 615 us -> 860 us (1.40)
  waiting for transfers between devices: 330 us -> 454 us
  local copies, waits for them, and re-layouts: 52.2 us -> 107 us
  starting transfers between devices: 54.6 us -> 94.4 us
  other arithmetic: 41.4 us -> 63 us
    ppermute x0 -> x15, waiting for transfers between devices: none -> 328 us  [the longest x8 328 us: collect(): lower.append(lax.ppermute(lower[-1] if lower else array, axis, pairs))]
    all_gather x1 -> x0, waiting for transfers between devices: 205 us -> none  [shards(): lax.all_gather(normed, 'exp', axis=0, tiled=True)]
    gather x0 -> x3, local copies, waits for them, and re-layouts: none -> 38 us  [collect(): parts = parts[(jnp.arange(size) - shift) % size]]
    ppermute x0 -> x15, starting transfers between devices: none -> 34 us  [the longest x7 33.9 us: collect(): upper.append(lax.ppermute(upper[-1] if upper else array, axis, back))]
    unnamed x2 -> x3, other arithmetic: 0.01 us -> 22.8 us
    unnamed x33 -> x96, local copies, waits for them, and re-layouts: 7.01 us -> 23.1 us
  transfers between devices with their start and end apart: 11 -> 25, of which waited for: 11 -> 18; matrix products, arithmetic and copies ran while one was open for 2% -> 2% of each run, Pallas kernels for 0% -> 0%
where the time goes in v1:
time: 860 us; the launch traced here: 853 us
  waiting for transfers between devices  454 us (53%)
  local copies, waits for them, and re-layouts  107 us (12%)
  starting transfers between devices  94.4 us (11%)
  blocking collectives  73.2 us (9%)
  other arithmetic  63 us (7%)
  matrix products  46.6 us (5%)
  between operations  14.3 us (2%)
    ppermute x8, waiting for transfers between devices, collect(): lower.append(lax.ppermute(lower[-1] if lower else array, axis, pairs))  328 us
    all_to_all x1, waiting for transfers between devices, shards(): lax.all_to_all(expert_rows, 'exp', split_axis=2, concat_axis=1, tiled=True)  100 us
    psum x1, blocking collectives, shards(): state_proj, dt_raw = lax.psum((state_part, rate_part), 'exp')  73.2 us
    ppermute x8, starting transfers between devices, passed_along(): lax.ppermute(value, axis, [(source, source + steps) for source in range(l...  52.7 us
    gather x3, local copies, waits for them, and re-layouts, collect(): parts = parts[(jnp.arange(size) - shift) % size]  38 us
    ppermute x7, starting transfers between devices, collect(): upper.append(lax.ppermute(upper[-1] if upper else array, axis, back))  33.9 us
    dot_general x1, matrix products, shards(): jnp.dot(collect(normed, 'exp', 0), in_weight, preferred_element_type=jnp....  23.8 us
    ppermute x8, waiting for transfers between devices, passed_along(): lax.ppermute(value, axis, [(source, source + steps) for source in range(l...  23.5 us
  transfers between devices with their start and end apart: 25, of which 18 were waited for; matrix products, arithmetic and copies ran while one was open for 2% of the time, Pallas kernels for 0%

profile of v1, /device:TPU:1, one launch (start us, length us, event | category | flops | bytes accessed | tf_op | source)
XLA Modules:
  0.0 853.2 jit_solution(3768130091586845297)
XLA Ops:
  6.5 7.8 all-to-all-start
  14.7 100.4 %all-to-all-done = bf16[1,1,16,24,8192]{4,3,1,0,2:T(8,128)(2,1)} async-done(((bf16[1,1,16,24,8192]{4,3,1,0,2:T(8,128)(2,1)}), bf16[1,1,16,24,8192]{4,3,1,0,2:T(8,128)(2,1)}, u32[]{:S(2)}, u32[]{:S(2)}) %all-to-all-start) | async-done | bytes 6291488 | tf_op jit(solution)/shard_map/all_to_all | solution.py:78
  115.1 12.7 %gather_fusion = bf16[256,8192]{1,0:T(8,128)(2,1)} fusion(bf16[384,8192]{1,0:T(8,128)(2,1)} %bitcast.3, s32[1024]{0:T(1024)S(1)} %pad_clamp_fusion.1), kind=kCustom, calls=%fused_computation | custom fusion | bytes 8389632 | tf_op jit(solution)/shard_map/jit(_take)/gather | solution.py:81
  127.8 8.1 reshape.147
  135.8 7.2 copy_select_fusion
  146.4 48.0 %collective-permute-done.1 = bf16[128,8192]{1,0:T(8,128)(2,1)S(1)} collective-permute-done((bf16[128,8192]{1,0:T(8,128)(2,1)S(1)}, bf16[128,8192]{1,0:T(8,128)(2,1)S(1)}, u32[]{:S(2)}, u32[]{:S(2)}) %collective-permute-start.1) | collective-permute-done | bytes 2097184 | tf_op jit(solution)/shard_map/ppermute | solution.py:26
  194.4 4.8 collective-permute-start.9
  199.1 42.3 %collective-permute-done.2 = bf16[128,8192]{1,0:T(8,128)(2,1)S(1)} collective-permute-done((bf16[128,8192]{1,0:T(8,128)(2,1)S(1)}, bf16[128,8192]{1,0:T(8,128)(2,1)S(1)}, u32[]{:S(2)}, u32[]{:S(2)}) %collective-permute-start.2) | collective-permute-done | bytes 2097184 | tf_op jit(solution)/shard_map/ppermute | solution.py:26
  241.4 4.8 collective-permute-start.10
  246.3 41.3 %collective-permute-done.3 = bf16[128,8192]{1,0:T(8,128)(2,1)S(1)} collective-permute-done((bf16[128,8192]{1,0:T(8,128)(2,1)S(1)}, bf16[128,8192]{1,0:T(8,128)(2,1)S(1)}, u32[]{:S(2)}, u32[]{:S(2)}) %collective-permute-start.3) | collective-permute-done | bytes 2097184 | tf_op jit(solution)/shard_map/ppermute | solution.py:26
  287.5 4.8 collective-permute-start.11
  292.4 40.3 %collective-permute-done.4 = bf16[128,8192]{1,0:T(8,128)(2,1)S(1)} collective-permute-done((bf16[128,8192]{1,0:T(8,128)(2,1)S(1)}, bf16[128,8192]{1,0:T(8,128)(2,1)S(1)}, u32[]{:S(2)}, u32[]{:S(2)}) %collective-permute-start.4) | collective-permute-done | bytes 2097184 | tf_op jit(solution)/shard_map/ppermute | solution.py:26
  332.7 5.0 collective-permute-start.12
  337.8 39.2 %collective-permute-done.5 = bf16[128,8192]{1,0:T(8,128)(2,1)S(1)} collective-permute-done((bf16[128,8192]{1,0:T(8,128)(2,1)S(1)}, bf16[128,8192]{1,0:T(8,128)(2,1)S(1)}, u32[]{:S(2)}, u32[]{:S(2)}) %collective-permute-start.5) | collective-permute-done | bytes 2097184 | tf_op jit(solution)/shard_map/ppermute | solution.py:26
  378.3 4.8 collective-permute-start.13
  383.1 38.0 %collective-permute-done.6 = bf16[128,8192]{1,0:T(8,128)(2,1)S(1)} collective-permute-done((bf16[128,8192]{1,0:T(8,128)(2,1)S(1)}, bf16[128,8192]{1,0:T(8,128)(2,1)S(1)}, u32[]{:S(2)}, u32[]{:S(2)}) %collective-permute-start.6) | collective-permute-done | bytes 2097184 | tf_op jit(solution)/shard_map/ppermute | solution.py:26
  421.1 4.8 collective-permute-start.14
  425.9 39.3 %collective-permute-done.7 = bf16[128,8192]{1,0:T(8,128)(2,1)} collective-permute-done((bf16[128,8192]{1,0:T(8,128)(2,1)S(1)}, bf16[128,8192]{1,0:T(8,128)(2,1)}, u32[]{:S(2)}, u32[]{:S(2)}) %collective-permute-start.7) | collective-permute-done | bytes 2097184 | tf_op jit(solution)/shard_map/ppermute | solution.py:26
  465.4 4.9 collective-permute-start.15
  470.2 39.2 %collective-permute-done.8 = bf16[128,8192]{1,0:T(8,128)(2,1)} collective-permute-done((bf16[128,8192]{1,0:T(8,128)(2,1)}, bf16[128,8192]{1,0:T(8,128)(2,1)}, u32[]{:S(2)}, u32[]{:S(2)}) %collective-permute-start.8) | collective-permute-done | bytes 2097184 | tf_op jit(solution)/shard_map/ppermute | solution.py:26
  524.4 11.8 %fusion.34 = (bf16[16,128,4096]{2,1,0:T(8,128)(2,1)}, bf16[16,128,4096]{2,1,0:T(8,128)(2,1)}) fusion(bf16[16,128,8192]{2,1,0:T(8,128)(2,1)S(1)} %bitcast_dynamic-update-slice_fusion.2), kind=kLoop, calls=%fused_computation.96 | loop fusion | bytes 67108864 | tf_op jit(solution)/shard_map/gather | solution.py:31
  536.2 13.1 %gather_fusion.1 = bf16[16,128,4096]{2,1,0:T(8,128)(2,1)} fusion(bf16[16,128,4096]{2,1,0:T(8,128)(2,1)} %get-tuple-element.255, s32[1024]{0:T(1024)S(1)} %pad_clamp_fusion), kind=kCustom, calls=%fused_computation.1 | custom fusion | bytes 33554496 | tf_op jit(solution)/shard_map/gather | solution.py:31
  549.3 13.1 %gather_fusion.2 = bf16[16,128,4096]{2,1,0:T(8,128)(2,1)} fusion(bf16[16,128,4096]{2,1,0:T(8,128)(2,1)} %get-tuple-element.256, s32[1024]{0:T(1024)S(1)} %pad_clamp_fusion), kind=kCustom, calls=%fused_computation.2 | custom fusion | bytes 33554496 | tf_op jit(solution)/shard_map/gather | solution.py:31
  562.4 22.8 %pad_maximum_fusion = bf16[16,128,8192]{2,1,0:T(8,128)(2,1)} fusion(bf16[16,128,4096]{2,1,0:T(8,128)(2,1)} %gather_fusion.2, bf16[16,128,4096]{2,1,0:T(8,128)(2,1)} %gather_fusion.1), kind=kLoop, calls=%fused_computation.45 | loop fusion | flops 67108864 | bytes 67108864
  585.2 23.8 %convolution_convert_fusion = bf16[2048,512]{1,0:T(8,128)(2,1)S(1)} fusion(bf16[2048,8192]{1,0:T(8,128)(2,1)} %bitcast.146, bf16[8192,512]{1,0:T(8,128)(2,1)} %param.24), kind=kOutput, calls=%fused_computation.55 | convolution fusion | flops 17180917760 | bytes 44040192 | tf_op jit(solution)/shard_map/dot_general | solution.py:92
  610.3 13.3 %collective-permute-start.16 = (bf16[3,512]{1,0:T(4,128)(2,1)S(1)}, bf16[3,512]{1,0:T(4,128)(2,1)S(1)}, u32[]{:S(2)}, u32[]{:S(2)}) collective-permute-start(bf16[3,512]{1,0:T(4,128)(2,1)S(1)} %slice.81), channel_id=1, source_target_pairs={{0,16},{16,32},{32,48},{48,64},{64,80},{80,96},{96,112},{1,17},{17... | collective-permute-start | bytes 9224 | tf_op jit(solution)/shard_map/ppermute | solution.py:38
  624.1 6.0 multiply_convert_fusion
  633.6 3.7 reshape.178
  637.3 4.0 copy.57
  641.3 73.2 %all-reduce.4 = bf16[2048,128]{1,0:T(8,128)(2,1)S(1)} all-reduce(f32[2048,128]{1,0:T(8,128)} %fusion.38), channel_id=1, replica_groups=mesh['seq'=8,'exp'=16] {'exp'}, use_global_device_ids=true, to_apply=%region_1.2 | all-reduce | flops 262144 | bytes 1572864 | tf_op jit(solution)/shard_map/psum | solution.py:105
  720.6 38.5 %while.34 = (s32[]{:T(128)}, f32[8,64,64]{1,2,0:T(8,128)S(1)}, f32[8]{0:T(128)S(1)}, f32[8,256,8]{1,2,0:T(8,128)}, f32[8,256,8,64]{1,3,2,0:T(8,128)}, /*index=5*...) while((s32[]{:T(128)}, f32[8,64,64]{1,2,0:T(8,128)S(1)}, ...), condition=%wide.region_6.7_spmd.clone, body=%wide.region_3.6_spmd.clone.sunk | while | flops 180033568 | bytes 2758157 | solution.py:131
  759.3 67.4 %while.33 = (s32[]{:T(128)}, f32[8,64,64]{2,1,0:T(8,128)}, f32[8,64,64]{2,1,0:T(8,128)S(1)}, f32[8]{0:T(128)S(1)}, f32[8,64,64]{2,1,0:T(8,128)S(1)}, /*index=5*/s32[]{:T(128)}) while((s32[]{:T(128)}, f32[8,64,64]{2,1,0:T(8,128)}, f32[8,64,64]{2,1,0:T(8,128)S(1)}, f32[8]{0:T(128)S(1)}, f32[8,64,64]{2,1,0:T(8,128)S(1)}, ...), condition=%wide.region_8.9_spmd, body=%wide.region_7.8_spmd.sunk | while | flops 65538 | bytes 1441961 | solution.py:149
  759.3 13.1 %collective-permute-start = (f32[8,64,64]{2,1,0:T(8,128)S(1)}, f32[8,64,64]{2,1,0:T(8,128)S(1)}, u32[]{:S(2)}, u32[]{:S(2)}) collective-permute-start(f32[8,64,64]{2,1,0:T(8,128)S(1)} %get-tuple-element.430), channel_id=1, source_target_pairs={{0,16},{16,32},{32,48},{48,64},{64,80},{80,96},{96,112},{1,17},{17... | collective-permute-start | bytes 393224 | tf_op jit(solution)/shard_map/while/body/eval_jaxpr/ppermute | solution.py:38
  772.4 3.3 collective-permute-done
  776.4 4.4 collective-permute-start
  780.8 3.3 collective-permute-done
  784.8 4.4 collective-permute-start
  789.2 3.3 collective-permute-done
  793.1 4.4 collective-permute-start
  797.5 3.3 collective-permute-done
  801.5 4.4 collective-permute-start
  805.9 3.3 collective-permute-done
  809.9 4.4 collective-permute-start
  814.3 3.3 collective-permute-done
  818.3 4.4 collective-permute-start
  822.6 3.3 collective-permute-done
  834.6 5.1 copy.67
  839.7 6.4 reshape.177
  (294 shorter events, 82.4 us)
Async XLA Ops:
  6.5 623.6 %copy-start = (bf16[512,128]{1,0:T(8,128)(2,1)S(1)}, bf16[512,128]{1,0:T(8,128)(2,1)}, u32[]{:S(2)}) copy-start(bf16[512,128]{1,0:T(8,128)(2,1)} %param.28) | copy-start | bytes 393220
  6.5 7.8 copy-start.34
  6.5 7.8 copy-start.35
  6.5 8.1 copy-start.36
  6.5 108.6 %all-to-all-start = ((bf16[1,1,16,24,8192]{4,3,1,0,2:T(8,128)(2,1)}), bf16[1,1,16,24,8192]{4,3,1,0,2:T(8,128)(2,1)}, u32[]{:S(2)}, u32[]{:S(2)}) async-start(bf16[1,1,16,24,8192]{4,3,1,0,2:T(8,128)(2,1)} %bitcast.149), calls=%async_computation | async-start | bytes 12582912 | tf_op jit(solution)/shard_map/all_to_all | solution.py:78
  14.3 705.3 %all-reduce.3.cloned.1.call-start = ((), (), s32[]{:S(2)}) async-start(), calls=%async_computation.1 | async-start | bytes 2097152 | tf_op jit(solution)/shard_map/psum | solution.py:105
  135.8 7.2 copy-start.2
  144.4 320.9 %copy-start.32 = (f32[4,512]{1,0:T(4,128)S(1)}, f32[4,512]{1,0:T(4,128)}, u32[]{:S(2)}) copy-start(f32[4,512]{1,0:T(4,128)} %param.25) | copy-start | bytes 24580
  146.3 48.1 %copy-start.3 = (bf16[128,8192]{1,0:T(8,128)(2,1)}, bf16[128,8192]{1,0:T(8,128)(2,1)S(1)}, u32[]{:S(2)}) copy-start(bf16[128,8192]{1,0:T(8,128)(2,1)S(1)} %multiply_convert_fusion.1) | copy-start | bytes 6291460
  146.3 48.0 %collective-permute-start.1 = (bf16[128,8192]{1,0:T(8,128)(2,1)S(1)}, bf16[128,8192]{1,0:T(8,128)(2,1)S(1)}, u32[]{:S(2)}, u32[]{:S(2)}) collective-permute-start(bf16[128,8192]{1,0:T(8,128)(2,1)S(1)} %multiply_convert_fusion.1), channel_id=1, source_target_pairs={{0,1},{1,2},{2,3},{3,4},{4,5},{5,6},{6,7},{7,8},{8,9},{9,10},{10,1... | collective-permute-start | bytes 6291464 | tf_op jit(solution)/shard_map/ppermute | solution.py:26
  194.3 47.1 %copy-start.7 = (bf16[128,8192]{1,0:T(8,128)(2,1)}, bf16[128,8192]{1,0:T(8,128)(2,1)S(1)}, u32[]{:S(2)}) copy-start(bf16[128,8192]{1,0:T(8,128)(2,1)S(1)} %collective-permute-done.1) | copy-start | bytes 6291460
  194.3 47.0 %collective-permute-start.2 = (bf16[128,8192]{1,0:T(8,128)(2,1)S(1)}, bf16[128,8192]{1,0:T(8,128)(2,1)S(1)}, u32[]{:S(2)}, u32[]{:S(2)}) collective-permute-start(bf16[128,8192]{1,0:T(8,128)(2,1)S(1)} %collective-permute-done.1), channel_id=1, source_target_pairs={{0,1},{1,2},{2,3},{3,4},{4,5},{5,6},{6,7},{7,8},{8,9},{9,10},{10,1... | collective-permute-start | bytes 6291464 | tf_op jit(solution)/shard_map/ppermute | solution.py:26
  194.4 47.0 %collective-permute-start.9 = (bf16[128,8192]{1,0:T(8,128)(2,1)S(1)}, bf16[128,8192]{1,0:T(8,128)(2,1)S(1)}, u32[]{:S(2)}, u32[]{:S(2)}) collective-permute-start(bf16[128,8192]{1,0:T(8,128)(2,1)S(1)} %multiply_convert_fusion.1), channel_id=1, source_target_pairs={{1,0},{2,1},{3,2},{4,3},{5,4},{6,5},{7,6},{8,7},{9,8},{10,9},{11,1... | collective-permute-start | bytes 6291464 | tf_op jit(solution)/shard_map/ppermute | solution.py:28
  241.4 46.1 %copy-start.11 = (bf16[128,8192]{1,0:T(8,128)(2,1)}, bf16[128,8192]{1,0:T(8,128)(2,1)S(1)}, u32[]{:S(2)}) copy-start(bf16[128,8192]{1,0:T(8,128)(2,1)S(1)} %collective-permute-done.2) | copy-start | bytes 6291460
  241.4 46.1 %collective-permute-start.3 = (bf16[128,8192]{1,0:T(8,128)(2,1)S(1)}, bf16[128,8192]{1,0:T(8,128)(2,1)S(1)}, u32[]{:S(2)}, u32[]{:S(2)}) collective-permute-start(bf16[128,8192]{1,0:T(8,128)(2,1)S(1)} %collective-permute-done.2), channel_id=1, source_target_pairs={{0,1},{1,2},{2,3},{3,4},{4,5},{5,6},{6,7},{7,8},{8,9},{9,10},{10,1... | collective-permute-start | bytes 6291464 | tf_op jit(solution)/shard_map/ppermute | solution.py:26
  241.4 4.8 copy-start.9
  241.4 46.1 %collective-permute-start.10 = (bf16[128,8192]{1,0:T(8,128)(2,1)S(1)}, bf16[128,8192]{1,0:T(8,128)(2,1)S(1)}, u32[]{:S(2)}, u32[]{:S(2)}) collective-permute-start(bf16[128,8192]{1,0:T(8,128)(2,1)S(1)} %collective-permute-done.9), channel_id=1, source_target_pairs={{1,0},{2,1},{3,2},{4,3},{5,4},{6,5},{7,6},{8,7},{9,8},{10,9},{11,1... | collective-permute-start | bytes 6291464 | tf_op jit(solution)/shard_map/ppermute | solution.py:28
  287.5 45.2 %copy-start.15 = (bf16[128,8192]{1,0:T(8,128)(2,1)}, bf16[128,8192]{1,0:T(8,128)(2,1)S(1)}, u32[]{:S(2)}) copy-start(bf16[128,8192]{1,0:T(8,128)(2,1)S(1)} %collective-permute-done.3) | copy-start | bytes 6291460
  287.5 45.2 %collective-permute-start.4 = (bf16[128,8192]{1,0:T(8,128)(2,1)S(1)}, bf16[128,8192]{1,0:T(8,128)(2,1)S(1)}, u32[]{:S(2)}, u32[]{:S(2)}) collective-permute-start(bf16[128,8192]{1,0:T(8,128)(2,1)S(1)} %collective-permute-done.3), channel_id=1, source_target_pairs={{0,1},{1,2},{2,3},{3,4},{4,5},{5,6},{6,7},{7,8},{8,9},{9,10},{10,1... | collective-permute-start | bytes 6291464 | tf_op jit(solution)/shard_map/ppermute | solution.py:26
  287.5 4.8 copy-start.13
  287.5 45.2 %collective-permute-start.11 = (bf16[128,8192]{1,0:T(8,128)(2,1)S(1)}, bf16[128,8192]{1,0:T(8,128)(2,1)S(1)}, u32[]{:S(2)}, u32[]{:S(2)}) collective-permute-start(bf16[128,8192]{1,0:T(8,128)(2,1)S(1)} %collective-permute-done.10), channel_id=1, source_target_pairs={{1,0},{2,1},{3,2},{4,3},{5,4},{6,5},{7,6},{8,7},{9,8},{10,9},{11,1... | collective-permute-start | bytes 6291464 | tf_op jit(solution)/shard_map/ppermute | solution.py:28
  332.7 88.4 %copy-start.21 = (bf16[128,8192]{1,0:T(8,128)(2,1)}, bf16[128,8192]{1,0:T(8,128)(2,1)S(1)}, u32[]{:S(2)}) copy-start(bf16[128,8192]{1,0:T(8,128)(2,1)S(1)} %collective-permute-done.4) | copy-start | bytes 6291460
  332.7 44.3 %collective-permute-start.5 = (bf16[128,8192]{1,0:T(8,128)(2,1)S(1)}, bf16[128,8192]{1,0:T(8,128)(2,1)S(1)}, u32[]{:S(2)}, u32[]{:S(2)}) collective-permute-start(bf16[128,8192]{1,0:T(8,128)(2,1)S(1)} %collective-permute-done.4), channel_id=1, source_target_pairs={{0,1},{1,2},{2,3},{3,4},{4,5},{5,6},{6,7},{7,8},{8,9},{9,10},{10,1... | collective-permute-start | bytes 6291464 | tf_op jit(solution)/shard_map/ppermute | solution.py:26
  332.7 5.0 copy-start.17
  332.7 44.3 %collective-permute-start.12 = (bf16[128,8192]{1,0:T(8,128)(2,1)S(1)}, bf16[128,8192]{1,0:T(8,128)(2,1)S(1)}, u32[]{:S(2)}, u32[]{:S(2)}) collective-permute-start(bf16[128,8192]{1,0:T(8,128)(2,1)S(1)} %collective-permute-done.11), channel_id=1, source_target_pairs={{1,0},{2,1},{3,2},{4,3},{5,4},{6,5},{7,6},{8,7},{9,8},{10,9},{11,1... | collective-permute-start | bytes 6291464 | tf_op jit(solution)/shard_map/ppermute | solution.py:28
  377.0 48.9 %copy-start.25 = (bf16[128,8192]{1,0:T(8,128)(2,1)}, bf16[128,8192]{1,0:T(8,128)(2,1)S(1)}, u32[]{:S(2)}) copy-start(bf16[128,8192]{1,0:T(8,128)(2,1)S(1)} %collective-permute-done.5) | copy-start | bytes 6291460
  377.0 44.1 %collective-permute-start.6 = (bf16[128,8192]{1,0:T(8,128)(2,1)S(1)}, bf16[128,8192]{1,0:T(8,128)(2,1)S(1)}, u32[]{:S(2)}, u32[]{:S(2)}) collective-permute-start(bf16[128,8192]{1,0:T(8,128)(2,1)S(1)} %collective-permute-done.5), channel_id=1, source_target_pairs={{0,1},{1,2},{2,3},{3,4},{4,5},{5,6},{6,7},{7,8},{8,9},{9,10},{10,1... | collective-permute-start | bytes 6291464 | tf_op jit(solution)/shard_map/ppermute | solution.py:26
  378.3 42.8 %collective-permute-start.13 = (bf16[128,8192]{1,0:T(8,128)(2,1)S(1)}, bf16[128,8192]{1,0:T(8,128)(2,1)S(1)}, u32[]{:S(2)}, u32[]{:S(2)}) collective-permute-start(bf16[128,8192]{1,0:T(8,128)(2,1)S(1)} %collective-permute-done.12), channel_id=1, source_target_pairs={{1,0},{2,1},{3,2},{4,3},{5,4},{6,5},{7,6},{8,7},{9,8},{10,9},{11,1... | collective-permute-start | bytes 6291464 | tf_op jit(solution)/shard_map/ppermute | solution.py:28
  421.1 44.2 %copy-start.27 = (bf16[128,8192]{1,0:T(8,128)(2,1)}, bf16[128,8192]{1,0:T(8,128)(2,1)S(1)}, u32[]{:S(2)}) copy-start(bf16[128,8192]{1,0:T(8,128)(2,1)S(1)} %collective-permute-done.6) | copy-start | bytes 6291460
  421.1 44.2 %collective-permute-start.7 = (bf16[128,8192]{1,0:T(8,128)(2,1)S(1)}, bf16[128,8192]{1,0:T(8,128)(2,1)}, u32[]{:S(2)}, u32[]{:S(2)}) collective-permute-start(bf16[128,8192]{1,0:T(8,128)(2,1)S(1)} %collective-permute-done.6), channel_id=1, source_target_pairs={{0,1},{1,2},{2,3},{3,4},{4,5},{5,6},{6,7},{7,8},{8,9},{9,10},{10,1... | collective-permute-start | bytes 6291464 | tf_op jit(solution)/shard_map/ppermute | solution.py:26
  421.1 49.1 %copy-start.23 = (bf16[128,8192]{1,0:T(8,128)(2,1)}, bf16[128,8192]{1,0:T(8,128)(2,1)S(1)}, u32[]{:S(2)}) copy-start(bf16[128,8192]{1,0:T(8,128)(2,1)S(1)} %collective-permute-done.13) | copy-start | bytes 6291460
  421.1 44.2 %collective-permute-start.14 = (bf16[128,8192]{1,0:T(8,128)(2,1)S(1)}, bf16[128,8192]{1,0:T(8,128)(2,1)}, u32[]{:S(2)}, u32[]{:S(2)}) collective-permute-start(bf16[128,8192]{1,0:T(8,128)(2,1)S(1)} %collective-permute-done.13), channel_id=1, source_target_pairs={{1,0},{2,1},{3,2},{4,3},{5,4},{6,5},{7,6},{8,7},{9,8},{10,9},{11,1... | collective-permute-start | bytes 6291464 | tf_op jit(solution)/shard_map/ppermute | solution.py:28
  465.3 44.1 %collective-permute-start.8 = (bf16[128,8192]{1,0:T(8,128)(2,1)}, bf16[128,8192]{1,0:T(8,128)(2,1)}, u32[]{:S(2)}, u32[]{:S(2)}) collective-permute-start(bf16[128,8192]{1,0:T(8,128)(2,1)} %collective-permute-done.7), channel_id=1, source_target_pairs={{0,1},{1,2},{2,3},{3,4},{4,5},{5,6},{6,7},{7,8},{8,9},{9,10},{10,1... | collective-permute-start | bytes 6291464 | tf_op jit(solution)/shard_map/ppermute | solution.py:26
  465.3 47.7 %copy-start.28 = (bf16[128,8192]{1,0:T(8,128)(2,1)S(1)}, bf16[128,8192]{1,0:T(8,128)(2,1)}, u32[]{:S(2)}) copy-start(bf16[128,8192]{1,0:T(8,128)(2,1)} %copy-done.27) | copy-start | bytes 6291460
  465.4 58.9 %collective-permute-start.15 = (bf16[128,8192]{1,0:T(8,128)(2,1)}, bf16[128,8192]{1,0:T(8,128)(2,1)S(1)}, u32[]{:S(2)}, u32[]{:S(2)}) collective-permute-start(bf16[128,8192]{1,0:T(8,128)(2,1)} %collective-permute-done.14), channel_id=1, source_target_pairs={{1,0},{2,1},{3,2},{4,3},{5,4},{6,5},{7,6},{8,7},{9,8},{10,9},{11,1... | collective-permute-start | bytes 6291464 | tf_op jit(solution)/shard_map/ppermute | solution.py:28
  511.1 2.2 copy-start.26
  585.2 38.4 %copy-start.39 = (f32[8]{0:T(128)S(1)}, f32[8]{0:T(128)}, u32[]{:S(2)}) copy-start(f32[8]{0:T(128)} %param.30) | copy-start | bytes 100
  585.2 39.0 %copy-start.33 = (f32[512]{0:T(512)S(1)}, f32[512]{0:T(512)}, u32[]{:S(2)}) copy-start(f32[512]{0:T(512)} %param.26) | copy-start | bytes 6148
  610.3 13.8 %collective-permute-start.16 = (bf16[3,512]{1,0:T(4,128)(2,1)S(1)}, bf16[3,512]{1,0:T(4,128)(2,1)S(1)}, u32[]{:S(2)}, u32[]{:S(2)}) collective-permute-start(bf16[3,512]{1,0:T(4,128)(2,1)S(1)} %slice.81), channel_id=1, source_target_pairs={{0,16},{16,32},{32,48},{48,64},{64,80},{80,96},{96,112},{1,17},{17... | collective-permute-start | bytes 9224 | tf_op jit(solution)/shard_map/ppermute | solution.py:38
  624.1 7.8 copy-start.29
  637.3 82.4 %copy-start.37 = (f32[8]{0:T(128)S(1)}, f32[8]{0:T(128)}, u32[]{:S(2)}) copy-start(f32[8]{0:T(128)} %param.29) | copy-start | bytes 100
  759.3 16.4 %collective-permute-start = (f32[8,64,64]{2,1,0:T(8,128)S(1)}, f32[8,64,64]{2,1,0:T(8,128)S(1)}, u32[]{:S(2)}, u32[]{:S(2)}) collective-permute-start(f32[8,64,64]{2,1,0:T(8,128)S(1)} %get-tuple-element.430), channel_id=1, source_target_pairs={{0,16},{16,32},{32,48},{48,64},{64,80},{80,96},{96,112},{1,17},{17... | collective-permute-start | bytes 393224 | tf_op jit(solution)/shard_map/while/body/eval_jaxpr/ppermute | solution.py:38
  776.4 7.7 collective-permute-start
  784.8 7.7 collective-permute-start
  793.1 7.7 collective-permute-start
  801.5 7.7 collective-permute-start
  809.9 7.7 collective-permute-start
  818.3 7.7 collective-permute-start
  (23 other events, 32.8 us)
Sparse Core Ops, SparseCore 0:
  632.1 87.5 all-reduce.2
